TPU v7x, 32 devices: a whole 2x2x4 slice. The times are simulated.
32 devices in a mesh: mom: 8 (over z, x), tm: 4 (over y, core).
Axes of the slice: x: 2, y: 2, z: 4, core: 2. Of those that a mesh axis runs over, the one named last changes fastest.
Arguments:
- new_rows: float32 [4, 256, 16, 512], P(None, 'mom', None, 'tm'), may hold values from -9 to 9
- history: float32 [3, 2, 256, 512, 512], P(None, None, 'mom', 'tm'), may hold values from -0.25 to 0.25
- momentum_map: int32 [256], replicated, may hold values from 0 to 255, each once
- step_index: int32 [1], replicated, may hold values from 0 to 999
- history_len: int32 [1], replicated, may hold values from 256 to 512
Outputs:
- advanced_rows: float32 [4, 256, 16, 512], P(None, 'mom', None, 'tm')
Inputs may be any that keep to these rules, and one draw needn't show every extreme that they name: `momentum_map`: each number of 0 to 255 appears once.
All inputs are finite; a program needn't handle non-finite values.
Results may differ from a plain program's by a relative error of at most 0.0003.
Values sent between devices are 32-bit elements; how exact they have to be, the bound alone decides.
A program may use at most 256 MiB of HBM per device.

v0:
```python
import jax
import jax.numpy as jnp
from jax import lax
from jax.sharding import PartitionSpec as P

SIDE = 16


TIME_STEP = 0.2
COUPLING = 5.0
DRIVE_RATE = 0.3
PRECISE = lax.Precision.HIGHEST


def lattice_tables(momentum_map, side):
    mom_count = momentum_map.shape[0]
    sites = jnp.arange(mom_count, dtype=jnp.int32)
    mom_x = momentum_map // side
    mom_y = momentum_map % side
    site_x = sites // side
    site_y = sites % side
    winding = (site_x[:, None] * mom_x[None, :] + site_y[:, None] * mom_y[None, :]) % side
    phases = winding.astype(jnp.float32) * (2.0 * jnp.pi / side)
    return (jnp.cos(phases), jnp.sin(phases))


def band_energy(own_map, row_times, side):
    wave_x = (own_map // side).astype(jnp.float32) * (2.0 * jnp.pi / side)
    wave_y = (own_map % side).astype(jnp.float32) * (2.0 * jnp.pi / side)
    drift = DRIVE_RATE * row_times
    return -2.0 * (
        jnp.cos(wave_x[:, None] + drift[None, :]) + jnp.cos(wave_y[:, None] + drift[None, :])
    )


def to_sites(cosine_table, sine_table, lattice):
    mom_count = lattice.shape[1]
    paired = lattice.reshape(2, 2, mom_count, lattice.shape[2])
    parts_re = paired[:, 0]
    parts_im = paired[:, 1]

    def apply_table(table, values):
        return jnp.einsum("rk,wkc->wrc", table, values, precision=PRECISE)

    site_re = (apply_table(cosine_table, parts_re) - apply_table(sine_table, parts_im)) / mom_count
    site_im = (apply_table(cosine_table, parts_im) + apply_table(sine_table, parts_re)) / mom_count
    return jnp.stack([site_re, site_im], axis=1).reshape(4, cosine_table.shape[0], lattice.shape[2])


def from_sites(cosine_table, sine_table, lattice):
    paired = lattice.reshape(2, 2, lattice.shape[1], lattice.shape[2])
    parts_re = paired[:, 0]
    parts_im = paired[:, 1]

    def apply_table(table, values):
        return jnp.einsum("rk,wrc->wkc", table, values, precision=PRECISE)

    mom_re = apply_table(cosine_table, parts_re) + apply_table(sine_table, parts_im)
    mom_im = apply_table(cosine_table, parts_im) - apply_table(sine_table, parts_re)
    return jnp.stack([mom_re, mom_im], axis=1).reshape(4, cosine_table.shape[1], lattice.shape[2])


def bubble_term(left_re, left_im, right_re, right_im):
    square_re = left_re * left_re - left_im * left_im
    square_im = 2.0 * left_re * left_im
    factor = -COUPLING * COUPLING
    return (
        factor * (square_re * right_re + square_im * right_im),
        factor * (square_im * right_re - square_re * right_im),
    )


def bubble(lattice):
    ret_re, ret_im, less_re, less_im = (lattice[0], lattice[1], lattice[2], lattice[3])
    great_re = less_re + ret_re
    great_im = less_im + ret_im
    lesser_re, lesser_im = bubble_term(less_re, less_im, great_re, great_im)
    greater_re, greater_im = bubble_term(great_re, great_im, less_re, less_im)
    return jnp.stack([greater_re - lesser_re, greater_im - lesser_im, lesser_re, lesser_im])


def contract(energy_pair, stored_pair):
    product = jnp.einsum("akiu,bkus->abkis", energy_pair, stored_pair, precision=PRECISE)
    return (product[0, 0] - product[1, 1], product[0, 1] + product[1, 0])


def memory_integral(self_energy, history):
    ret_ret = contract(self_energy[0:2], history[0])
    ret_less = contract(self_energy[0:2], history[1])
    less_adv = contract(self_energy[2:4], history[2])
    return TIME_STEP * jnp.stack(
        [ret_ret[0], ret_ret[1], ret_less[0] + less_adv[0], ret_less[1] + less_adv[1]]
    )


def rotate(total):
    return jnp.stack([total[1], -total[0], total[3], -total[2]])


def body(new_rows, history, momentum_map, step_index, history_len):
    own_count = new_rows.shape[1]
    row_count = new_rows.shape[2]
    time_count = new_rows.shape[3]
    cosine_table, sine_table = lattice_tables(momentum_map, SIDE)
    mom_start = lax.axis_index("mom") * own_count
    own_map = lax.dynamic_slice_in_dim(momentum_map, mom_start, own_count, 0)
    time_start = lax.axis_index("tm") * time_count
    positions = time_start + jnp.arange(time_count, dtype=jnp.int32)
    memory_mask = (positions < history_len[0]).astype(jnp.float32)
    first_times = step_index[0].astype(jnp.float32) + jnp.arange(row_count, dtype=jnp.int32).astype(
        jnp.float32
    )

    def slope(estimate, offset_steps):
        band = band_energy(own_map, (first_times + offset_steps) * TIME_STEP, SIDE)
        flattened = estimate.reshape(4, own_count, row_count * time_count)
        by_site = lax.all_to_all(flattened, "mom", split_axis=2, concat_axis=1, tiled=True)
        site_energy = from_sites(
            cosine_table, sine_table, bubble(to_sites(cosine_table, sine_table, by_site))
        )
        returned = lax.all_to_all(site_energy, "mom", split_axis=1, concat_axis=2, tiled=True)
        self_energy = returned.reshape(4, own_count, row_count, time_count)
        self_energy = self_energy * memory_mask
        partial_rows = memory_integral(self_energy, history)
        integral = lax.psum_scatter(partial_rows, "tm", scatter_dimension=3, tiled=True)
        return rotate(band[None, :, :, None] * estimate + integral)

    current = new_rows
    for time_step in range(2):
        slope_now = slope(current, float(time_step))
        estimate = current + TIME_STEP * slope_now
        for corrector in range(2):
            estimate = current + 0.5 * TIME_STEP * (
                slope_now + slope(estimate, float(time_step + 1))
            )
        current = estimate
    return current


def solution(mesh):
    in_specs = (P(None, "mom", None, "tm"), P(None, None, "mom", "tm", None), P(), P(), P())
    out_specs = P(None, "mom", None, "tm")
    return jax.shard_map(body, mesh=mesh, in_specs=in_specs, out_specs=out_specs, check_vma=False)
```

profile of v0, /device:TPU:0, one launch (start us, length us, event | category | flops | bytes accessed | tf_op | source)
XLA Modules:
  0.0 1199.9 jit_solution(13687722654620009129)
XLA Ops:
  23.6 33.7 %fusion.513 = (f32[1,2,32,128,512]{4,3,2,1,0:T(8,128)}, f32[1,2,32,128,512]{4,3,2,1,0:T(8,128)}, f32[1,2,32,128,512]{4,3,2,1,0:T(8,128)}) fusion(f32[3,2,32,128,512]{4,3,2,1,0:T(8,128)} %param.6), kind=kLoop, calls=%fused_computation.673 | loop fusion | bytes 100663296 | tf_op jit(solution)/shard_map/slice | solution.py:88
  92.5 21.9 %copy_bitcast_fusion = (f32[2,32,128,512,1]{3,2,0,1,4:T(8,128)}, f32[2,32,128,512,1]{3,2,0,1,4:T(8,128)}) fusion(f32[1,2,32,128,512]{4,3,2,1,0:T(8,128)} %get-tuple-element.45, f32[1,2,32,128,512]{4,3,2,1,0:T(8,128)} %get-tuple-element.44), kind=kLoop, calls=%fused_computation | loop fusion | bytes 67108864 | tf_op jit(solution)/shard_map/squeeze | solution.py:90
  119.9 12.4 %fusion.88 = f32[2,2,32,16,512]{4,3,1,0,2:T(8,128)S(1)} fusion(f32[1,2,32,128,512]{4,3,2,1,0:T(8,128)} %get-tuple-element.43, f32[4,32,16,128]{3,2,0,1:T(8,128)S(1)} %broadcast_multiply_fusion.5), kind=kOutput, calls=%fused_computation.63 | convolution fusion | flops 1610612736 | bytes 21495808 | tf_op jit(solution)/shard_map/akiu,bkus->abkis/dot_general | solution.py:83
  132.9 10.0 fusion.55
  142.9 10.1 fusion.37
  158.4 41.6 %reduce-scatter.7.cloned.1.call-done = f32[4,32,16,128]{3,2,1,0:T(8,128)} async-done(((f32[4,32,16,512]{3,2,1,0:T(8,128)}), f32[4,32,16,128]{3,2,1,0:T(8,128)}) %reduce-scatter.7.cloned.1.call-update) | async-done | bytes 1048592 | tf_op jit(solution)/shard_map/reduce_scatter | solution.py:125
  208.9 31.0 %all_to_all.180 = f32[8,1,32768]{2,1,0:T(1,128)} all-to-all(f32[8,1,32768]{2,1,0:T(1,128)S(1)} %reshape.1100), channel_id=1, replica_groups=mesh['mom'=8,'tm'=4] {'mom'}, dimensions={0} | all-to-all | bytes 2097152 | tf_op jit(solution)/shard_map/all_to_all | solution.py:117
  274.3 28.9 %all_to_all.181 = f32[4,256,256]{2,0,1:T(4,128)S(1)} all-to-all(f32[4,256,256]{2,0,1:T(4,128)S(1)} %copy.286), channel_id=1, replica_groups=mesh['mom'=8,'tm'=4] {'mom'}, dimensions={1} | all-to-all | bytes 2097152 | tf_op jit(solution)/shard_map/all_to_all | solution.py:121
  306.5 13.9 %fusion.40 = f32[2,2,32,16,512]{4,3,2,1,0:T(8,128)} fusion(f32[2,32,128,512,1]{3,2,0,1,4:T(8,128)} %get-tuple-element.110, f32[2,32,16,128,1]{3,2,0,1,4:T(8,128)S(1)} %get-tuple-element.96), kind=kOutput, calls=%fused_computation.47 | convolution fusion | flops 1610612736 | bytes 21495808 | tf_op jit(solution)/shard_map/akiu,bkus->abkis/dot_general | solution.py:83
  320.5 10.5 fusion.73
  331.1 9.6 fusion.58
  346.8 42.5 %reduce-scatter.9.cloned.1.call-done = f32[4,32,16,128]{3,2,1,0:T(8,128)} async-done(((f32[4,32,16,512]{3,2,1,0:T(8,128)}), f32[4,32,16,128]{3,2,1,0:T(8,128)}) %reduce-scatter.9.cloned.1.call-update) | async-done | bytes 1048592 | tf_op jit(solution)/shard_map/reduce_scatter | solution.py:125
  399.3 31.0 %all_to_all.182 = f32[8,1,32768]{2,1,0:T(1,128)} all-to-all(f32[8,1,32768]{2,1,0:T(1,128)S(1)} %reshape.1102), channel_id=1, replica_groups=mesh['mom'=8,'tm'=4] {'mom'}, dimensions={0} | all-to-all | bytes 2097152 | tf_op jit(solution)/shard_map/all_to_all | solution.py:117
  464.5 28.9 %all_to_all.183 = f32[4,256,256]{2,0,1:T(4,128)S(1)} all-to-all(f32[4,256,256]{2,0,1:T(4,128)S(1)} %copy.301), channel_id=1, replica_groups=mesh['mom'=8,'tm'=4] {'mom'}, dimensions={1} | all-to-all | bytes 2097152 | tf_op jit(solution)/shard_map/all_to_all | solution.py:121
  496.6 11.6 fusion.43
  508.3 11.8 fusion.76
  533.8 42.5 %reduce-scatter.11.cloned.1.call-done = f32[4,32,16,128]{3,2,1,0:T(8,128)} async-done(((f32[4,32,16,512]{3,2,1,0:T(8,128)}), f32[4,32,16,128]{3,2,1,0:T(8,128)}) %reduce-scatter.11.cloned.1.call-update) | async-done | bytes 1048592 | tf_op jit(solution)/shard_map/reduce_scatter | solution.py:125
  588.1 31.2 %all_to_all.184 = f32[8,1,32768]{2,1,0:T(1,128)} all-to-all(f32[8,1,32768]{2,1,0:T(1,128)} %reshape.1104), channel_id=1, replica_groups=mesh['mom'=8,'tm'=4] {'mom'}, dimensions={0} | all-to-all | bytes 2097152 | tf_op jit(solution)/shard_map/all_to_all | solution.py:117
  665.6 28.9 %all_to_all.185 = f32[4,256,256]{2,0,1:T(4,128)S(1)} all-to-all(f32[4,256,256]{2,0,1:T(4,128)S(1)} %copy.316), channel_id=1, replica_groups=mesh['mom'=8,'tm'=4] {'mom'}, dimensions={1} | all-to-all | bytes 2097152 | tf_op jit(solution)/shard_map/all_to_all | solution.py:121
  700.0 11.6 fusion.46
  711.6 12.1 %fusion.79 = f32[2,2,32,16,512]{4,3,2,1,0:T(8,128)S(1)} fusion(f32[2,32,16,128,1]{3,2,0,1,4:T(8,128)S(1)} %get-tuple-element.84, f32[1,2,32,128,512]{4,3,2,1,0:T(8,128)} %get-tuple-element.43), kind=kOutput, calls=%fused_computation.60 | convolution fusion | flops 1610612736 | bytes 21495808 | tf_op jit(solution)/shard_map/akiu,bkus->abkis/dot_general | solution.py:83
  737.3 42.5 %reduce-scatter.13.cloned.1.call-done = f32[4,32,16,128]{3,2,1,0:T(8,128)} async-done(((f32[4,32,16,512]{3,2,1,0:T(8,128)}), f32[4,32,16,128]{3,2,1,0:T(8,128)}) %reduce-scatter.13.cloned.1.call-update) | async-done | bytes 1048592 | tf_op jit(solution)/shard_map/reduce_scatter | solution.py:125
  792.6 31.2 %all_to_all.186 = f32[8,1,32768]{2,1,0:T(1,128)} all-to-all(f32[8,1,32768]{2,1,0:T(1,128)} %reshape.1106), channel_id=1, replica_groups=mesh['mom'=8,'tm'=4] {'mom'}, dimensions={0} | all-to-all | bytes 2097152 | tf_op jit(solution)/shard_map/all_to_all | solution.py:117
  870.1 28.9 %all_to_all.187 = f32[4,256,256]{2,0,1:T(4,128)S(1)} all-to-all(f32[4,256,256]{2,0,1:T(4,128)S(1)} %copy.332), channel_id=1, replica_groups=mesh['mom'=8,'tm'=4] {'mom'}, dimensions={1} | all-to-all | bytes 2097152 | tf_op jit(solution)/shard_map/all_to_all | solution.py:121
  904.5 11.6 fusion.49
  916.1 11.8 fusion.82
  942.3 41.9 %reduce-scatter.15.cloned.1.call-done = f32[4,32,16,128]{3,2,1,0:T(8,128)} async-done(((f32[4,32,16,512]{3,2,1,0:T(8,128)}), f32[4,32,16,128]{3,2,1,0:T(8,128)}) %reduce-scatter.15.cloned.1.call-update) | async-done | bytes 1048592 | tf_op jit(solution)/shard_map/reduce_scatter | solution.py:125
  997.5 31.2 %all_to_all.188 = f32[8,1,32768]{2,1,0:T(1,128)} all-to-all(f32[8,1,32768]{2,1,0:T(1,128)} %reshape.1108), channel_id=1, replica_groups=mesh['mom'=8,'tm'=4] {'mom'}, dimensions={0} | all-to-all | bytes 2097152 | tf_op jit(solution)/shard_map/all_to_all | solution.py:117
  1075.0 28.9 %all_to_all.189 = f32[4,256,256]{2,0,1:T(4,128)S(1)} all-to-all(f32[4,256,256]{2,0,1:T(4,128)S(1)} %copy.347), channel_id=1, replica_groups=mesh['mom'=8,'tm'=4] {'mom'}, dimensions={1} | all-to-all | bytes 2097152 | tf_op jit(solution)/shard_map/all_to_all | solution.py:121
  1109.3 11.6 fusion.52
  1121.0 11.9 fusion.85
  1146.5 42.6 %reduce-scatter.17.cloned.1.call-done = f32[4,32,16,128]{3,2,1,0:T(8,128)} async-done(((f32[4,32,16,512]{3,2,1,0:T(8,128)}), f32[4,32,16,128]{3,2,1,0:T(8,128)}) %reduce-scatter.17.cloned.1.call-update) | async-done | bytes 1048592 | tf_op jit(solution)/shard_map/reduce_scatter | solution.py:125
  (351 shorter events, 413.2 us)
Async XLA Ops:
  10.2 12.7 %copy-start.26 = (s32[256]{0:T(256)S(1)}, s32[256]{0:T(256)}, u32[]{:S(2)}) copy-start(s32[256]{0:T(256)} %param.7) | copy-start | bytes 3076
  15.6 41.7 %all-to-all-start = ((f32[8,1,32768]{2,1,0:T(1,128)}), f32[8,1,32768]{2,1,0:T(1,128)S(1)}, u32[]{:S(2)}, u32[]{:S(2)}) async-start(f32[8,1,32768]{2,1,0:T(1,128)} %reshape.1098), calls=%async_computation | async-start | bytes 2097152 | tf_op jit(solution)/shard_map/all_to_all | solution.py:117
  86.4 31.4 %all-to-all-start.1 = ((f32[4,256,256]{2,0,1:T(4,128)}), f32[4,256,256]{2,0,1:T(4,128)S(1)}, u32[]{:S(2)}, u32[]{:S(2)}) async-start(f32[4,256,256]{2,0,1:T(4,128)} %copy.266), calls=%async_computation.1 | async-start | bytes 2097152 | tf_op jit(solution)/shard_map/all_to_all | solution.py:121
  92.4 107.6 %reduce-scatter.7.cloned.1.call-start = ((), (), s32[]{:S(2)}) async-start(), calls=%async_computation.18 | async-start | bytes 5242880 | tf_op jit(solution)/shard_map/reduce_scatter | solution.py:125
  119.9 12.9 %slice-start.4 = ((s8[16777216]{0:T(1024)(128)(4,1)}), s8[4194304]{0:T(1024)(128)(4,1)S(1)}, s32[]{:S(2)}) async-start(s8[16777216]{0:T(1024)(128)(4,1)} %bitcast.598), calls=%async_computation.28 | async-start | bytes 8388608
  119.9 12.9 %slice-start.5 = ((s8[16777216]{0:T(1024)(128)(4,1)}), s8[4194304]{0:T(1024)(128)(4,1)S(1)}, s32[]{:S(2)}) async-start(s8[16777216]{0:T(1024)(128)(4,1)} %bitcast.598), calls=%async_computation.29 | async-start | bytes 8388608
  119.9 12.9 %slice-start.6 = ((s8[16777216]{0:T(1024)(128)(4,1)}), s8[4194304]{0:T(1024)(128)(4,1)S(1)}, s32[]{:S(2)}) async-start(s8[16777216]{0:T(1024)(128)(4,1)} %bitcast.598), calls=%async_computation.30 | async-start | bytes 8388608
  119.9 12.9 %slice-start.7 = ((s8[16777216]{0:T(1024)(128)(4,1)}), s8[4194304]{0:T(1024)(128)(4,1)S(1)}, s32[]{:S(2)}) async-start(s8[16777216]{0:T(1024)(128)(4,1)} %bitcast.598), calls=%async_computation.31 | async-start | bytes 8388608
  156.6 43.4 %copy-start = (f32[4,32,16,128]{3,2,1,0:T(8,128)S(1)}, f32[4,32,16,128]{3,2,1,0:T(8,128)}, u32[]{:S(2)}) copy-start(f32[4,32,16,128]{3,2,1,0:T(8,128)} %param.5) | copy-start | bytes 3145732
  156.7 232.6 %reduce-scatter.9.cloned.1.call-start = ((), (), s32[]{:S(2)}) async-start(), calls=%async_computation.19 | async-start | bytes 5242880 | tf_op jit(solution)/shard_map/reduce_scatter | solution.py:125
  306.2 14.2 %slice-start = ((s8[16777216]{0:T(1024)(128)(4,1)}), s8[4194304]{0:T(1024)(128)(4,1)S(1)}, s32[]{:S(2)}) async-start(s8[16777216]{0:T(1024)(128)(4,1)} %bitcast.596), calls=%async_computation.24 | async-start | bytes 8388608
  306.4 14.0 %slice-start.1 = ((s8[16777216]{0:T(1024)(128)(4,1)}), s8[4194304]{0:T(1024)(128)(4,1)S(1)}, s32[]{:S(2)}) async-start(s8[16777216]{0:T(1024)(128)(4,1)} %bitcast.596), calls=%async_computation.25 | async-start | bytes 8388608
  306.4 14.0 %slice-start.2 = ((s8[16777216]{0:T(1024)(128)(4,1)}), s8[4194304]{0:T(1024)(128)(4,1)S(1)}, s32[]{:S(2)}) async-start(s8[16777216]{0:T(1024)(128)(4,1)} %bitcast.596), calls=%async_computation.26 | async-start | bytes 8388608
  306.5 14.0 %slice-start.3 = ((s8[16777216]{0:T(1024)(128)(4,1)}), s8[4194304]{0:T(1024)(128)(4,1)S(1)}, s32[]{:S(2)}) async-start(s8[16777216]{0:T(1024)(128)(4,1)} %bitcast.596), calls=%async_computation.27 | async-start | bytes 8388608
  306.5 24.6 %slice-start.8 = ((s8[16777216]{0:T(1024)(128)(4,1)}), s8[4194304]{0:T(1024)(128)(4,1)S(1)}, s32[]{:S(2)}) async-start(s8[16777216]{0:T(1024)(128)(4,1)} %bitcast.600), calls=%async_computation.32 | async-start | bytes 8388608
  306.5 24.6 %slice-start.9 = ((s8[16777216]{0:T(1024)(128)(4,1)}), s8[4194304]{0:T(1024)(128)(4,1)S(1)}, s32[]{:S(2)}) async-start(s8[16777216]{0:T(1024)(128)(4,1)} %bitcast.600), calls=%async_computation.33 | async-start | bytes 8388608
  346.6 229.7 %reduce-scatter.11.cloned.1.call-start = ((), (), s32[]{:S(2)}) async-start(), calls=%async_computation.20 | async-start | bytes 5242880 | tf_op jit(solution)/shard_map/reduce_scatter | solution.py:125
  496.6 23.5 %slice-start.12 = ((s8[16777216]{0:T(1024)(128)(4,1)}), s8[4194304]{0:T(1024)(128)(4,1)S(1)}, s32[]{:S(2)}) async-start(s8[16777216]{0:T(1024)(128)(4,1)} %bitcast.602), calls=%async_computation.36 | async-start | bytes 8388608
  496.6 23.5 %slice-start.13 = ((s8[16777216]{0:T(1024)(128)(4,1)}), s8[4194304]{0:T(1024)(128)(4,1)S(1)}, s32[]{:S(2)}) async-start(s8[16777216]{0:T(1024)(128)(4,1)} %bitcast.602), calls=%async_computation.37 | async-start | bytes 8388608
  533.7 42.6 %copy-start.17 = (f32[1,32,16,128]{3,2,1,0:T(8,128)S(1)}, f32[1,32,16,128]{3,2,1,0:T(8,128)}, u32[]{:S(2)}) copy-start(f32[1,32,16,128]{3,2,1,0:T(8,128)} %copy-done.16) | copy-start | bytes 786436
  533.7 42.6 %copy-start.19 = (f32[1,32,16,128]{3,2,1,0:T(8,128)S(1)}, f32[1,32,16,128]{3,2,1,0:T(8,128)}, u32[]{:S(2)}) copy-start(f32[1,32,16,128]{3,2,1,0:T(8,128)} %copy-done.18) | copy-start | bytes 786436
  533.7 42.6 %copy-start.21 = (f32[1,32,16,128]{3,2,1,0:T(8,128)S(1)}, f32[1,32,16,128]{3,2,1,0:T(8,128)}, u32[]{:S(2)}) copy-start(f32[1,32,16,128]{3,2,1,0:T(8,128)} %copy-done.20) | copy-start | bytes 786436
  533.8 246.1 %reduce-scatter.13.cloned.1.call-start = ((), (), s32[]{:S(2)}) async-start(), calls=%async_computation.21 | async-start | bytes 5242880 | tf_op jit(solution)/shard_map/reduce_scatter | solution.py:125
  699.9 23.8 %slice-start.16 = ((s8[16777216]{0:T(1024)(128)(4,1)}), s8[4194304]{0:T(1024)(128)(4,1)S(1)}, s32[]{:S(2)}) async-start(s8[16777216]{0:T(1024)(128)(4,1)} %bitcast.604), calls=%async_computation.40 | async-start | bytes 8388608
  700.0 23.8 %slice-start.17 = ((s8[16777216]{0:T(1024)(128)(4,1)}), s8[4194304]{0:T(1024)(128)(4,1)S(1)}, s32[]{:S(2)}) async-start(s8[16777216]{0:T(1024)(128)(4,1)} %bitcast.604), calls=%async_computation.41 | async-start | bytes 8388608
  711.6 12.1 %slice-start.18 = ((s8[16777216]{0:T(1024)(128)(4,1)}), s8[4194304]{0:T(1024)(128)(4,1)S(1)}, s32[]{:S(2)}) async-start(s8[16777216]{0:T(1024)(128)(4,1)} %bitcast.604), calls=%async_computation.42 | async-start | bytes 8388608
  737.3 246.9 %reduce-scatter.15.cloned.1.call-start = ((), (), s32[]{:S(2)}) async-start(), calls=%async_computation.22 | async-start | bytes 5242880 | tf_op jit(solution)/shard_map/reduce_scatter | solution.py:125
  904.5 23.5 %slice-start.20 = ((s8[16777216]{0:T(1024)(128)(4,1)}), s8[4194304]{0:T(1024)(128)(4,1)S(1)}, s32[]{:S(2)}) async-start(s8[16777216]{0:T(1024)(128)(4,1)} %bitcast.606), calls=%async_computation.44 | async-start | bytes 8388608
  904.5 23.5 %slice-start.21 = ((s8[16777216]{0:T(1024)(128)(4,1)}), s8[4194304]{0:T(1024)(128)(4,1)S(1)}, s32[]{:S(2)}) async-start(s8[16777216]{0:T(1024)(128)(4,1)} %bitcast.606), calls=%async_computation.45 | async-start | bytes 8388608
  941.6 247.5 %reduce-scatter.17.cloned.1.call-start = ((), (), s32[]{:S(2)}) async-start(), calls=%async_computation.23 | async-start | bytes 5242880 | tf_op jit(solution)/shard_map/reduce_scatter | solution.py:125
  1109.3 23.6 %slice-start.24 = ((s8[16777216]{0:T(1024)(128)(4,1)}), s8[4194304]{0:T(1024)(128)(4,1)S(1)}, s32[]{:S(2)}) async-start(s8[16777216]{0:T(1024)(128)(4,1)} %bitcast.608), calls=%async_computation.48 | async-start | bytes 8388608
  1109.3 23.6 %slice-start.25 = ((s8[16777216]{0:T(1024)(128)(4,1)}), s8[4194304]{0:T(1024)(128)(4,1)S(1)}, s32[]{:S(2)}) async-start(s8[16777216]{0:T(1024)(128)(4,1)} %bitcast.608), calls=%async_computation.49 | async-start | bytes 8388608
  (35 other events, 208.2 us)
Sparse Core Ops, SparseCore 0:
  156.8 43.2 reduce-scatter.6
  346.8 42.4 reduce-scatter.8
  533.9 42.4 reduce-scatter.10
  737.4 42.4 reduce-scatter.12
  941.7 42.4 reduce-scatter.14
  1146.6 42.4 reduce-scatter.16
where the time goes:
time: 1210 us; the launch traced here: 1200 us
  matrix products  300 us (25%)
  blocking collectives  300 us (25%)
  waiting for transfers between devices  257 us (21%)
  local copies, waits for them, and re-layouts  219 us (18%)
  other arithmetic  92.8 us (8%)
  between operations  17 us (1%)
  starting transfers between devices  13.5 us (1%)
    reduce_scatter x6, waiting for transfers between devices, slope(): lax.psum_scatter(partial_rows, 'tm', scatter_dimension=3, tiled=True)  254 us
    dot_general x18, matrix products, contract(): jnp.einsum('akiu,bkus->abkis', energy_pair, stored_pair, precision=PRECISE)  197 us
    all_to_all x5, blocking collectives, slope(): lax.all_to_all(flattened, 'mom', split_axis=2, concat_axis=1, tiled=True)  156 us
    all_to_all x5, blocking collectives, slope(): lax.all_to_all(site_energy, 'mom', split_axis=1, concat_axis=2, tiled=True)  144 us
    unnamed x131, local copies, waits for them, and re-layouts  67.9 us
    dot_general x24, matrix products, apply_table(): return jnp.einsum('rk,wkc->wrc', table, values, precision=PRECISE)  55.1 us
    dot_general x24, matrix products, apply_table(): return jnp.einsum('rk,wrc->wkc', table, values, precision=PRECISE)  48.2 us
    slice x7, local copies, waits for them, and re-layouts, memory_integral(): ret_ret = contract(self_energy[0:2], history[0])  35.2 us
  transfers between devices with their start and end apart: 8, of which 7 were waited for; matrix products, arithmetic and copies ran while one was open for 5% of the time, Pallas kernels for 0%

commit v1 on v0

--- a/solution.py
+++ b/solution.py
@@ -1,7 +1,12 @@
+import functools
+
 import jax
 import jax.numpy as jnp
 from jax import lax
+from jax.experimental import pallas as pl
+from jax.experimental.pallas import tpu as pltpu
 from jax.sharding import PartitionSpec as P
+
 
 SIDE = 16
 
@@ -137,7 +142,361 @@
     return current
 
 
+MESH = pl.DeviceIdType.MESH
+CHUNKS = 4
+
+
+def halves(values):
+    high = values.astype(jnp.bfloat16)
+    return high, (values - high.astype(jnp.float32)).astype(jnp.bfloat16)
+
+
+def product(left, right):
+    return jnp.dot(left, right, preferred_element_type=jnp.float32)
+
+
+def triple(left_high, left_low, right):
+    right_high, right_low = halves(right)
+    return (
+        product(left_high, right_high)
+        + product(left_high, right_low)
+        + product(left_low, right_high)
+    )
+
+
+def integral_kernel(
+    mom_size,
+    slots,
+    state_ref,
+    mask_ref,
+    site_high,
+    site_low,
+    back_high,
+    back_low,
+    history_ref,
+    out_ref,
+    outgoing,
+    gathered,
+    energy,
+    returned,
+    partial,
+    core_rows,
+    chip_rows,
+    stored,
+    stored_sem,
+    row_send,
+    row_recv,
+    energy_send,
+    energy_recv,
+    core_send,
+    core_recv,
+    chip_send,
+    chip_recv,
+):
+    mom = lax.axis_index("mom")
+    tm = lax.axis_index("tm")
+    core = tm % 2
+    chip = tm // 2
+    near = chip * 2 + (1 - core)
+    far = (1 - chip) * 2 + core
+    _, own, rows, times = out_ref.shape
+    share = rows // mom_size
+    sites = gathered.shape[2]
+    chunk = own // CHUNKS
+
+    def fetch(index, slot):
+        return pltpu.make_async_copy(
+            history_ref.at[:, :, index], stored.at[slot], stored_sem.at[slot]
+        )
+
+    for slot in range(slots):
+        fetch(slot, slot).start()
+
+    barrier = pltpu.get_barrier_semaphore()
+    for step in range(1, mom_size):
+        pl.semaphore_signal(
+            barrier, inc=1, device_id={"mom": (mom + step) % mom_size}, device_id_type=MESH
+        )
+    for peer in (near, far):
+        pl.semaphore_signal(barrier, inc=1, device_id={"tm": peer}, device_id_type=MESH)
+
+    @pl.loop(0, rows)
+    def _(row):
+        for part in range(4):
+            outgoing[row, part] = state_ref[pl.ds(part * own * rows + row, own, stride=rows), :]
+
+    pl.semaphore_wait(barrier, mom_size + 1)
+
+    def row_copy(line, step):
+        peer = (mom + step) % mom_size
+        return pltpu.make_async_remote_copy(
+            src_ref=outgoing.at[peer * share + line],
+            dst_ref=gathered.at[line, :, pl.ds(pl.multiple_of(mom * own, own), own), :],
+            send_sem=row_send.at[line, step],
+            recv_sem=row_recv.at[line, step],
+            device_id={"mom": peer},
+            device_id_type=MESH,
+        )
+
+    def landing(line):
+        depth = 4 * own
+        return pl.ds(pl.multiple_of((mom * share + line) * depth, depth), depth)
+
+    def energy_copy(line, step):
+        peer = (mom + step) % mom_size
+        return pltpu.make_async_remote_copy(
+            src_ref=energy.at[line, peer],
+            dst_ref=returned.at[landing(line)],
+            send_sem=energy_send.at[line, step],
+            recv_sem=energy_recv.at[line, step],
+            device_id={"mom": peer},
+            device_id_type=MESH,
+        )
+
+    for line in range(share):
+        for step in range(1, mom_size):
+            row_copy(line, step).start()
+    mine = pl.ds(pl.multiple_of(mom * own, own), own)
+    for line in range(share):
+        gathered[line, :, mine, :] = outgoing[mom * share + line]
+
+    mask = mask_ref[0:1, :]
+
+    @pl.loop(0, share)
+    def _(line):
+        for step in range(1, mom_size):
+            row_copy(line, step).wait_recv()
+        fields = []
+        for pair in range(2):
+            both = jnp.concatenate(
+                [gathered[line, 2 * pair], gathered[line, 2 * pair + 1]], axis=1
+            )
+            turned = triple(site_high[...], site_low[...], both)
+            fields.append((turned[:sites, :times] - turned[sites:, times:]) / sites)
+            fields.append((turned[:sites, times:] + turned[sites:, :times]) / sites)
+        ret_re, ret_im, less_re, less_im = fields
+        great_re = less_re + ret_re
+        great_im = less_im + ret_im
+        lesser_re, lesser_im = bubble_term(less_re, less_im, great_re, great_im)
+        greater_re, greater_im = bubble_term(great_re, great_im, less_re, less_im)
+        pairs = (
+            (greater_re - lesser_re, greater_im - lesser_im),
+            (lesser_re, lesser_im),
+        )
+        for pair, (part_re, part_im) in enumerate(pairs):
+            both = jnp.concatenate([part_re, part_im], axis=1)
+            turned = triple(back_high[...], back_low[...], both)
+            mom_re = (turned[:sites, :times] + turned[sites:, times:]) * mask
+            mom_im = (turned[:sites, times:] - turned[sites:, :times]) * mask
+            for part, values in ((2 * pair, mom_re), (2 * pair + 1, mom_im)):
+                for peer in range(mom_size):
+                    energy[line, peer, part * own : (part + 1) * own] = values[
+                        peer * own : (peer + 1) * own
+                    ]
+        for step in range(1, mom_size):
+            energy_copy(line, step).start()
+        returned[landing(line)] = energy[line, mom]
+
+    for line in range(share):
+        for step in range(1, mom_size):
+            energy_copy(line, step).wait_recv()
+
+    def one_momentum(index):
+        slot = index % slots
+        fetch(index, slot).wait()
+        ret_re, ret_im, less_re, less_im = [
+            returned[pl.ds(part * own + index, rows, stride=4 * own), :] for part in range(4)
+        ]
+
+        def folded(part_re, part_im):
+            return jnp.concatenate(
+                [
+                    jnp.concatenate([part_re, -part_im], axis=1),
+                    jnp.concatenate([part_im, part_re], axis=1),
+                ],
+                axis=0,
+            )
+
+        def applied(high, both, kind):
+            weights_high, weights_low = halves(stored[slot, kind].reshape(2 * times, -1))
+            stacked = product(both, weights_high)
+            return stacked[: 2 * rows] + stacked[2 * rows :] + product(high, weights_low)
+
+        ret_high, ret_low = halves(folded(ret_re, ret_im))
+        ret_both = jnp.concatenate([ret_high, ret_low], axis=0)
+        less_high, less_low = halves(folded(less_re, less_im))
+        less_both = jnp.concatenate([less_high, less_low], axis=0)
+        ret_sum = applied(ret_high, ret_both, 0)
+        less_sum = applied(ret_high, ret_both, 1) + applied(less_high, less_both, 2)
+        for block in range(4):
+            window = slice(block * times, (block + 1) * times)
+            partial[block, index, : 2 * rows] = TIME_STEP * ret_sum[:, window]
+            partial[block, index, 2 * rows :] = TIME_STEP * less_sum[:, window]
+
+        @pl.when(index + slots < own)
+        def _():
+            fetch(index + slots, slot).start()
+
+    def core_copy(piece, side):
+        span = pl.ds(piece * chunk, chunk)
+        return pltpu.make_async_remote_copy(
+            src_ref=partial.at[2 * side + (1 - core), span],
+            dst_ref=core_rows.at[side, span],
+            send_sem=core_send.at[side, piece],
+            recv_sem=core_recv.at[side, piece],
+            device_id={"tm": near},
+            device_id_type=MESH,
+        )
+
+    def chip_copy(piece):
+        span = pl.ds(piece * chunk, chunk)
+        return pltpu.make_async_remote_copy(
+            src_ref=partial.at[2 * (1 - chip) + core, span],
+            dst_ref=chip_rows.at[span],
+            send_sem=chip_send.at[piece],
+            recv_sem=chip_recv.at[piece],
+            device_id={"tm": far},
+            device_id_type=MESH,
+        )
+
+    @pl.loop(0, CHUNKS + 2)
+    def _(turn):
+        @pl.when(turn < CHUNKS)
+        def _():
+            @pl.loop(0, chunk)
+            def _(inner):
+                one_momentum(turn * chunk + inner)
+
+            for side in range(2):
+                core_copy(turn, side).start()
+
+        @pl.when((turn >= 1) & (turn <= CHUNKS))
+        def _():
+            piece = turn - 1
+            span = pl.ds(piece * chunk, chunk)
+            for side in range(2):
+                core_copy(piece, side).wait_recv()
+                block = 2 * side + core
+                partial[block, span] = partial[block, span] + core_rows[side, span]
+            chip_copy(piece).start()
+
+        @pl.when(turn >= 2)
+        def _():
+            piece = turn - 2
+            span = pl.ds(piece * chunk, chunk)
+            chip_copy(piece).wait_recv()
+            total = partial[2 * chip + core, span] + chip_rows[span]
+            for part in range(4):
+                out_ref[part, span] = total[:, part * rows : (part + 1) * rows, :]
+
+    for line in range(share):
+        for step in range(1, mom_size):
+            row_copy(line, step).wait_send()
+            energy_copy(line, step).wait_send()
+    for piece in range(CHUNKS):
+        for side in range(2):
+            core_copy(piece, side).wait_send()
+        chip_copy(piece).wait_send()
+
+
+def fits(mesh_sizes, new_rows):
+    _, own_count, row_count, time_count = new_rows.shape
+    return (
+        mesh_sizes["tm"] == 4
+        and row_count % mesh_sizes["mom"] == 0
+        and row_count % 8 == 0
+        and own_count % 8 == 0
+        and time_count % 128 == 0
+    )
+
+
+def slope_integral(mom_size, estimate, mask_rows, tables, history):
+    parts, own, rows, times = estimate.shape
+    sites = own * mom_size
+    full = history.shape[4]
+    share = rows // mom_size
+    slots = min(16, own)
+    vmem = pl.BlockSpec(memory_space=pltpu.VMEM)
+    dma = pltpu.SemaphoreType.DMA
+    f32 = jnp.float32
+    return pl.pallas_call(
+        functools.partial(integral_kernel, mom_size, slots),
+        out_shape=jax.ShapeDtypeStruct(estimate.shape, f32),
+        in_specs=[vmem] * 6 + [pl.BlockSpec(memory_space=pl.ANY)],
+        out_specs=vmem,
+        scratch_shapes=[
+            pltpu.VMEM((rows, parts, own, times), f32),
+            pltpu.VMEM((share, parts, sites, times), f32),
+            pltpu.VMEM((share, mom_size, parts * own, times), f32),
+            pltpu.VMEM((rows * parts * own, times), f32),
+            pltpu.VMEM((4, own, parts * rows, times), f32),
+            pltpu.VMEM((2, own, parts * rows, times), f32),
+            pltpu.VMEM((own, parts * rows, times), f32),
+            pltpu.VMEM((slots, 3, 2, times, full), f32),
+            dma((slots,)),
+            dma((share, mom_size)),
+            dma((share, mom_size)),
+            dma((share, mom_size)),
+            dma((share, mom_size)),
+            dma((2, CHUNKS)),
+            dma((2, CHUNKS)),
+            dma((CHUNKS,)),
+            dma((CHUNKS,)),
+        ],
+        compiler_params=pltpu.CompilerParams(
+            collective_id=0, has_side_effects=True, vmem_limit_bytes=56 * 1024 * 1024
+        ),
+        name="slope_integral",
+    )(estimate.reshape(parts * own * rows, times), mask_rows, *tables, history)
+
+
+def table_halves(table):
+    high = lax.reduce_precision(table, exponent_bits=8, mantissa_bits=7)
+    return high.astype(jnp.bfloat16), (table - high).astype(jnp.bfloat16)
+
+
+def fused_body(mom_size, new_rows, history, momentum_map, step_index, history_len):
+    own_count = new_rows.shape[1]
+    row_count = new_rows.shape[2]
+    time_count = new_rows.shape[3]
+    cosine_table, sine_table = lattice_tables(momentum_map, SIDE)
+    tables = table_halves(jnp.concatenate([cosine_table, sine_table], axis=0)) + table_halves(
+        jnp.concatenate([cosine_table.T, sine_table.T], axis=0)
+    )
+    own_map = lax.dynamic_slice_in_dim(momentum_map, lax.axis_index("mom") * own_count, own_count, 0)
+    positions = lax.axis_index("tm") * time_count + jnp.arange(time_count, dtype=jnp.int32)
+    memory_mask = (positions < history_len[0]).astype(jnp.float32)
+    mask_rows = jnp.broadcast_to(memory_mask[None, :], (8, time_count))
+    first_times = step_index[0].astype(jnp.float32) + jnp.arange(row_count, dtype=jnp.int32).astype(
+        jnp.float32
+    )
+
+    def slope(estimate, offset_steps):
+        band = band_energy(own_map, (first_times + offset_steps) * TIME_STEP, SIDE)
+        integral = slope_integral(mom_size, estimate, mask_rows, tables, history)
+        return rotate(band[None, :, :, None] * estimate + integral)
+
+    current = new_rows
+    for time_step in range(2):
+        slope_now = slope(current, float(time_step))
+        estimate = current + TIME_STEP * slope_now
+        for corrector in range(2):
+            estimate = current + 0.5 * TIME_STEP * (
+                slope_now + slope(estimate, float(time_step + 1))
+            )
+        current = estimate
+    return current
+
+
 def solution(mesh):
     in_specs = (P(None, "mom", None, "tm"), P(None, None, "mom", "tm", None), P(), P(), P())
     out_specs = P(None, "mom", None, "tm")
-    return jax.shard_map(body, mesh=mesh, in_specs=in_specs, out_specs=out_specs, check_vma=False)
+
+    def dispatch(new_rows, *others):
+        if fits(dict(mesh.shape), new_rows):
+            return fused_body(mesh.shape["mom"], new_rows, *others)
+        return body(new_rows, *others)
+
+    return jax.shard_map(
+        dispatch, mesh=mesh, in_specs=in_specs, out_specs=out_specs, check_vma=False
+    )

time: 1210 us -> 512 us (0.42)
  Pallas kernels: 0 us -> 487 us
  matrix products: 300 us -> 0 us
  blocking collectives: 300 us -> 0 us
  waiting for transfers between devices: 257 us -> 0 us
  local copies, waits for them, and re-layouts: 219 us -> 0.82 us
  other arithmetic: 92.8 us -> 22.2 us
  between operations: 17 us -> 1.59 us
  starting transfers between devices: 13.5 us -> 0 us
    pallas_call x0 -> x6, Pallas kernels: none -> 487 us  [slope_integral(): pl.pallas_call(functools.partial(integral_kernel, mom_size, slots), out_s...]
    dot_general x66 -> x0, matrix products: 300 us -> none  [the longest x18 197 us: contract(): jnp.einsum('akiu,bkus->abkis', energy_pair, stored_pair, precision=PRECISE)]
    all_to_all x10 -> x0, blocking collectives: 300 us -> none  [the longest x5 156 us: slope(): lax.all_to_all(flattened, 'mom', split_axis=2, concat_axis=1, tiled=True)]
    reduce_scatter x6 -> x0, waiting for transfers between devices: 254 us -> none  [slope(): lax.psum_scatter(partial_rows, 'tm', scatter_dimension=3, tiled=True)]
    unnamed x131 -> x2, local copies, waits for them, and re-layouts: 67.9 us -> 0.01 us
    reshape x17 -> x0, local copies, waits for them, and re-layouts: 36.9 us -> none  [the longest x5 16.3 us: slope(): flattened = estimate.reshape(4, own_count, row_count * time_count)]
    all_to_all x19 -> x0, local copies, waits for them, and re-layouts: 35.8 us -> none  [the longest x7 26.1 us: slope(): lax.all_to_all(flattened, 'mom', split_axis=2, concat_axis=1, tiled=True)]
    slice x7 -> x0, local copies, waits for them, and re-layouts: 35.2 us -> none  [memory_integral(): ret_ret = contract(self_energy[0:2], history[0])]
  transfers between devices with their start and end apart: 8 -> 0, of which waited for: 7 -> 0; matrix products, arithmetic and copies ran while one was open for 5% -> 0% of each run, Pallas kernels for 0% -> 0%
where the time goes in v1:
time: 512 us; the launch traced here: 511 us
  Pallas kernels  487 us (95%)
  other arithmetic  22.2 us (4%)
    pallas_call x6, Pallas kernels, slope_integral(): pl.pallas_call(functools.partial(integral_kernel, mom_size, slots), out_s...  487 us

profile of v1, /device:TPU:0, one launch (start us, length us, event | category | flops | bytes accessed | tf_op | source)
XLA Modules:
  0.0 511.2 jit_solution(481044678302474814)
XLA Ops:
  1.4 0.8 convert_multiply_fusion
  2.2 0.7 and_select_fusion.2
  2.9 0.6 broadcast_in_dim.2.mask_ref
  3.5 0.2 add_multiply_fusion
  3.8 0.1 copy.8
  3.8 0.1 copy.7
  4.0 2.2 fusion.17
  6.2 1.1 fusion.8
  7.3 82.6 %slope_integral.6 = f32[4,32,16,128]{3,2,1,0:T(8,128)} custom-call(f32[2048,128]{1,0:T(8,128)} %bitcast.9, f32[8,128]{1,0:T(8,128)} %broadcast_in_dim.2.mask_ref, bf16[512,256]{1,0:T(8,128)(2,1)} %get-tuple-element.34.site_high, bf16[512,256]{1,0:T(8,128)(2,1)} %get-tuple-element.33.site_low, bf16[512,256]{1,0:T(8,128)(2,1)} %get-tuple-element.44.back_high, ...), custom_call_target="tpu_custom_call" | custom-call | tf_op jit(solution)/shard_map/slope_integral/pallas_call | solution.py:422
  89.9 1.4 multiply_add_fusion.7
  91.3 0.1 fusion.30
  91.4 1.1 multiply_add_fusion.6
  92.5 81.3 %slope_integral.7 = f32[4,32,16,128]{3,2,1,0:T(8,128)} custom-call(f32[2048,128]{1,0:T(8,128)} %bitcast.10, f32[8,128]{1,0:T(8,128)} %broadcast_in_dim.2.mask_ref, bf16[512,256]{1,0:T(8,128)(2,1)} %get-tuple-element.34.site_high, bf16[512,256]{1,0:T(8,128)(2,1)} %get-tuple-element.33.site_low, bf16[512,256]{1,0:T(8,128)(2,1)} %get-tuple-element.44.back_high, ...), custom_call_target="tpu_custom_call" | custom-call | tf_op jit(solution)/shard_map/slope_integral/pallas_call | solution.py:422
  173.8 1.5 multiply_add_fusion.5
  175.3 0.1 fusion.29
  175.4 1.2 fusion.1
  176.5 81.5 %slope_integral.8 = f32[4,32,16,128]{3,2,1,0:T(8,128)} custom-call(f32[2048,128]{1,0:T(8,128)} %bitcast.13, f32[8,128]{1,0:T(8,128)} %broadcast_in_dim.2.mask_ref, bf16[512,256]{1,0:T(8,128)(2,1)} %get-tuple-element.34.site_high, bf16[512,256]{1,0:T(8,128)(2,1)} %get-tuple-element.33.site_low, bf16[512,256]{1,0:T(8,128)(2,1)} %get-tuple-element.44.back_high, ...), custom_call_target="tpu_custom_call" | custom-call | tf_op jit(solution)/shard_map/slope_integral/pallas_call | solution.py:422
  258.0 1.5 multiply_add_fusion.4
  259.6 0.1 fusion.28
  259.7 1.2 fusion.3
  260.8 80.5 %slope_integral.9 = f32[4,32,16,128]{3,2,1,0:T(8,128)} custom-call(f32[2048,128]{1,0:T(8,128)} %bitcast.14, f32[8,128]{1,0:T(8,128)} %broadcast_in_dim.2.mask_ref, bf16[512,256]{1,0:T(8,128)(2,1)} %get-tuple-element.34.site_high, bf16[512,256]{1,0:T(8,128)(2,1)} %get-tuple-element.33.site_low, bf16[512,256]{1,0:T(8,128)(2,1)} %get-tuple-element.44.back_high, ...), custom_call_target="tpu_custom_call" | custom-call | tf_op jit(solution)/shard_map/slope_integral/pallas_call | solution.py:422
  341.3 1.5 multiply_add_fusion.3
  342.8 0.1 fusion.27
  342.9 1.2 multiply_add_fusion.2
  344.2 80.5 %slope_integral.10 = f32[4,32,16,128]{3,2,1,0:T(8,128)} custom-call(f32[2048,128]{1,0:T(8,128)} %bitcast.11, f32[8,128]{1,0:T(8,128)} %broadcast_in_dim.2.mask_ref, bf16[512,256]{1,0:T(8,128)(2,1)} %get-tuple-element.34.site_high, bf16[512,256]{1,0:T(8,128)(2,1)} %get-tuple-element.33.site_low, bf16[512,256]{1,0:T(8,128)(2,1)} %get-tuple-element.44.back_high, ...), custom_call_target="tpu_custom_call" | custom-call | tf_op jit(solution)/shard_map/slope_integral/pallas_call | solution.py:422
  424.7 1.6 multiply_add_fusion.1
  426.3 0.1 fusion.26
  426.4 1.3 fusion.5
  427.7 80.3 %slope_integral.11 = f32[4,32,16,128]{3,2,1,0:T(8,128)} custom-call(f32[2048,128]{1,0:T(8,128)} %bitcast.12, f32[8,128]{1,0:T(8,128)} %broadcast_in_dim.2.mask_ref, bf16[512,256]{1,0:T(8,128)(2,1)} %get-tuple-element.34.site_high, bf16[512,256]{1,0:T(8,128)(2,1)} %get-tuple-element.33.site_low, bf16[512,256]{1,0:T(8,128)(2,1)} %get-tuple-element.44.back_high, ...), custom_call_target="tpu_custom_call" | custom-call | tf_op jit(solution)/shard_map/slope_integral/pallas_call | solution.py:422
  508.1 1.7 multiply_add_fusion
  509.8 0.1 fusion.25
  509.8 1.4 fusion.7
  (9 shorter events, 0.1 us)
Async XLA Ops:
  0.0 89.9 %copy-start = (f32[4,32,16,128]{3,2,1,0:T(8,128)S(1)}, f32[4,32,16,128]{3,2,1,0:T(8,128)}, u32[]{:S(2)}) copy-start(f32[4,32,16,128]{3,2,1,0:T(8,128)} %param.5) | copy-start | bytes 3145732

commit v2 on v1

--- a/solution.py
+++ b/solution.py
@@ -143,7 +143,7 @@
 
 
 MESH = pl.DeviceIdType.MESH
-CHUNKS = 4
+CHUNKS = 8
 
 
 def halves(values):
@@ -230,7 +230,7 @@
     def row_copy(line, step):
         peer = (mom + step) % mom_size
         return pltpu.make_async_remote_copy(
-            src_ref=outgoing.at[peer * share + line],
+            src_ref=outgoing.at[line * mom_size + peer],
             dst_ref=gathered.at[line, :, pl.ds(pl.multiple_of(mom * own, own), own), :],
             send_sem=row_send.at[line, step],
             recv_sem=row_recv.at[line, step],
@@ -240,7 +240,7 @@
 
     def landing(line):
         depth = 4 * own
-        return pl.ds(pl.multiple_of((mom * share + line) * depth, depth), depth)
+        return pl.ds(pl.multiple_of((line * mom_size + mom) * depth, depth), depth)
 
     def energy_copy(line, step):
         peer = (mom + step) % mom_size
@@ -258,7 +258,7 @@
             row_copy(line, step).start()
     mine = pl.ds(pl.multiple_of(mom * own, own), own)
     for line in range(share):
-        gathered[line, :, mine, :] = outgoing[mom * share + line]
+        gathered[line, :, mine, :] = outgoing[line * mom_size + mom]
 
     mask = mask_ref[0:1, :]
 
@@ -297,15 +297,20 @@
             energy_copy(line, step).start()
         returned[landing(line)] = energy[line, mom]
 
-    for line in range(share):
-        for step in range(1, mom_size):
-            energy_copy(line, step).wait_recv()
-
-    def one_momentum(index):
-        slot = index % slots
-        fetch(index, slot).wait()
+    def one_momentum(line, step):
+        load = step - line * slots
+        index = load % own
+        slot = load % slots
+
+        @pl.when((line == 0) | (load >= own))
+        def _():
+            fetch(index, slot).wait()
+
         ret_re, ret_im, less_re, less_im = [
-            returned[pl.ds(part * own + index, rows, stride=4 * own), :] for part in range(4)
+            returned[
+                pl.ds(line * mom_size * 4 * own + part * own + index, mom_size, stride=4 * own), :
+            ]
+            for part in range(4)
         ]
 
         def folded(part_re, part_im):
@@ -320,7 +325,7 @@
         def applied(high, both, kind):
             weights_high, weights_low = halves(stored[slot, kind].reshape(2 * times, -1))
             stacked = product(both, weights_high)
-            return stacked[: 2 * rows] + stacked[2 * rows :] + product(high, weights_low)
+            return stacked[: 2 * mom_size] + stacked[2 * mom_size :] + product(high, weights_low)
 
         ret_high, ret_low = halves(folded(ret_re, ret_im))
         ret_both = jnp.concatenate([ret_high, ret_low], axis=0)
@@ -330,70 +335,82 @@
         less_sum = applied(ret_high, ret_both, 1) + applied(less_high, less_both, 2)
         for block in range(4):
             window = slice(block * times, (block + 1) * times)
-            partial[block, index, : 2 * rows] = TIME_STEP * ret_sum[:, window]
-            partial[block, index, 2 * rows :] = TIME_STEP * less_sum[:, window]
-
-        @pl.when(index + slots < own)
+            partial[line, block, index, : 2 * mom_size] = TIME_STEP * ret_sum[:, window]
+            partial[line, block, index, 2 * mom_size :] = TIME_STEP * less_sum[:, window]
+
+        @pl.when(load + slots < own + line * (own - slots))
         def _():
-            fetch(index + slots, slot).start()
-
-    def core_copy(piece, side):
-        span = pl.ds(piece * chunk, chunk)
+            fetch((load + slots) % own, slot).start()
+
+    def place(turn):
+        line = turn // CHUNKS
+        return line, pl.ds((turn * chunk - line * slots) % own, chunk)
+
+    def core_copy(turn, side):
+        line, span = place(turn)
         return pltpu.make_async_remote_copy(
-            src_ref=partial.at[2 * side + (1 - core), span],
-            dst_ref=core_rows.at[side, span],
-            send_sem=core_send.at[side, piece],
-            recv_sem=core_recv.at[side, piece],
+            src_ref=partial.at[line, 2 * side + (1 - core), span],
+            dst_ref=core_rows.at[line, side, span],
+            send_sem=core_send.at[side, turn],
+            recv_sem=core_recv.at[side, turn],
             device_id={"tm": near},
             device_id_type=MESH,
         )
 
-    def chip_copy(piece):
-        span = pl.ds(piece * chunk, chunk)
+    def chip_copy(turn):
+        line, span = place(turn)
         return pltpu.make_async_remote_copy(
-            src_ref=partial.at[2 * (1 - chip) + core, span],
-            dst_ref=chip_rows.at[span],
-            send_sem=chip_send.at[piece],
-            recv_sem=chip_recv.at[piece],
+            src_ref=partial.at[line, 2 * (1 - chip) + core, span],
+            dst_ref=chip_rows.at[line, span],
+            send_sem=chip_send.at[turn],
+            recv_sem=chip_recv.at[turn],
             device_id={"tm": far},
             device_id_type=MESH,
         )
 
-    @pl.loop(0, CHUNKS + 2)
+    turns = share * CHUNKS
+
+    @pl.loop(0, turns + 2)
     def _(turn):
-        @pl.when(turn < CHUNKS)
+        @pl.when(turn < turns)
         def _():
+            line = turn // CHUNKS
+
+            @pl.when(turn % CHUNKS == 0)
+            def _():
+                for step in range(1, mom_size):
+                    energy_copy(line, step).wait_recv()
+
             @pl.loop(0, chunk)
             def _(inner):
-                one_momentum(turn * chunk + inner)
+                one_momentum(line, turn * chunk + inner)
 
             for side in range(2):
                 core_copy(turn, side).start()
 
-        @pl.when((turn >= 1) & (turn <= CHUNKS))
+        @pl.when((turn >= 1) & (turn <= turns))
         def _():
-            piece = turn - 1
-            span = pl.ds(piece * chunk, chunk)
+            line, span = place(turn - 1)
             for side in range(2):
-                core_copy(piece, side).wait_recv()
+                core_copy(turn - 1, side).wait_recv()
                 block = 2 * side + core
-                partial[block, span] = partial[block, span] + core_rows[side, span]
-            chip_copy(piece).start()
+                partial[line, block, span] = partial[line, block, span] + core_rows[line, side, span]
+            chip_copy(turn - 1).start()
 
         @pl.when(turn >= 2)
         def _():
-            piece = turn - 2
-            span = pl.ds(piece * chunk, chunk)
-            chip_copy(piece).wait_recv()
-            total = partial[2 * chip + core, span] + chip_rows[span]
+            line, span = place(turn - 2)
+            chip_copy(turn - 2).wait_recv()
+            total = partial[line, 2 * chip + core, span] + chip_rows[line, span]
+            group = pl.ds(pl.multiple_of(line * mom_size, mom_size), mom_size)
             for part in range(4):
-                out_ref[part, span] = total[:, part * rows : (part + 1) * rows, :]
+                out_ref[part, span, group, :] = total[:, part * mom_size : (part + 1) * mom_size, :]
 
     for line in range(share):
         for step in range(1, mom_size):
             row_copy(line, step).wait_send()
             energy_copy(line, step).wait_send()
-    for piece in range(CHUNKS):
+    for piece in range(turns):
         for side in range(2):
             core_copy(piece, side).wait_send()
         chip_copy(piece).wait_send()
@@ -403,9 +420,9 @@
     _, own_count, row_count, time_count = new_rows.shape
     return (
         mesh_sizes["tm"] == 4
-        and row_count % mesh_sizes["mom"] == 0
-        and row_count % 8 == 0
-        and own_count % 8 == 0
+        and mesh_sizes["mom"] % 8 == 0
+        and row_count == 2 * mesh_sizes["mom"]
+        and own_count % CHUNKS == 0
         and time_count % 128 == 0
     )
 
@@ -415,7 +432,7 @@
     sites = own * mom_size
     full = history.shape[4]
     share = rows // mom_size
-    slots = min(16, own)
+    slots = own - own // CHUNKS
     vmem = pl.BlockSpec(memory_space=pltpu.VMEM)
     dma = pltpu.SemaphoreType.DMA
     f32 = jnp.float32
@@ -429,22 +446,22 @@
             pltpu.VMEM((share, parts, sites, times), f32),
             pltpu.VMEM((share, mom_size, parts * own, times), f32),
             pltpu.VMEM((rows * parts * own, times), f32),
-            pltpu.VMEM((4, own, parts * rows, times), f32),
-            pltpu.VMEM((2, own, parts * rows, times), f32),
-            pltpu.VMEM((own, parts * rows, times), f32),
+            pltpu.VMEM((share, 4, own, parts * mom_size, times), f32),
+            pltpu.VMEM((share, 2, own, parts * mom_size, times), f32),
+            pltpu.VMEM((share, own, parts * mom_size, times), f32),
             pltpu.VMEM((slots, 3, 2, times, full), f32),
             dma((slots,)),
             dma((share, mom_size)),
             dma((share, mom_size)),
             dma((share, mom_size)),
             dma((share, mom_size)),
-            dma((2, CHUNKS)),
-            dma((2, CHUNKS)),
-            dma((CHUNKS,)),
-            dma((CHUNKS,)),
+            dma((2, share * CHUNKS)),
+            dma((2, share * CHUNKS)),
+            dma((share * CHUNKS,)),
+            dma((share * CHUNKS,)),
         ],
         compiler_params=pltpu.CompilerParams(
-            collective_id=0, has_side_effects=True, vmem_limit_bytes=56 * 1024 * 1024
+            collective_id=0, has_side_effects=True, vmem_limit_bytes=60 * 1024 * 1024
         ),
         name="slope_integral",
     )(estimate.reshape(parts * own * rows, times), mask_rows, *tables, history)

time: 512 us -> 569 us (1.11)
  Pallas kernels: 487 us -> 535 us
    pallas_call x6, Pallas kernels: 487 us -> 535 us  [slope_integral(): pl.pallas_call(functools.partial(integral_kernel, mom_size, slots), out_s...]
where the time goes in v2:
time: 569 us; the launch traced here: 564 us
  Pallas kernels  535 us (94%)
  other arithmetic  24.5 us (4%)
    pallas_call x6, Pallas kernels, slope_integral(): pl.pallas_call(functools.partial(integral_kernel, mom_size, slots), out_s...  535 us

profile of v2, /device:TPU:0, one launch (start us, length us, event | category | flops | bytes accessed | tf_op | source)
XLA Modules:
  0.0 563.5 jit_solution(12698869911586739104)
XLA Ops:
  1.4 0.8 convert_multiply_fusion
  2.2 0.7 and_select_fusion.2
  2.9 0.6 broadcast_in_dim.2.mask_ref
  3.5 0.2 add_multiply_fusion
  4.0 2.2 fusion.17
  6.2 1.1 fusion.8
  7.4 84.9 %slope_integral.6 = f32[4,32,16,128]{3,2,1,0:T(8,128)} custom-call(f32[2048,128]{1,0:T(8,128)} %bitcast.9, f32[8,128]{1,0:T(8,128)} %broadcast_in_dim.2.mask_ref, bf16[512,256]{1,0:T(8,128)(2,1)} %get-tuple-element.34.site_high, bf16[512,256]{1,0:T(8,128)(2,1)} %get-tuple-element.33.site_low, bf16[512,256]{1,0:T(8,128)(2,1)} %get-tuple-element.44.back_high, ...), custom_call_target="tpu_custom_call" | custom-call | tf_op jit(solution)/shard_map/slope_integral/pallas_call | solution.py:439
  92.2 1.4 multiply_add_fusion.7
  93.7 0.1 fusion.30
  93.7 1.1 multiply_add_fusion.6
  94.9 90.2 %slope_integral.7 = f32[4,32,16,128]{3,2,1,0:T(8,128)} custom-call(f32[2048,128]{1,0:T(8,128)} %bitcast.10, f32[8,128]{1,0:T(8,128)} %broadcast_in_dim.2.mask_ref, bf16[512,256]{1,0:T(8,128)(2,1)} %get-tuple-element.34.site_high, bf16[512,256]{1,0:T(8,128)(2,1)} %get-tuple-element.33.site_low, bf16[512,256]{1,0:T(8,128)(2,1)} %get-tuple-element.44.back_high, ...), custom_call_target="tpu_custom_call" | custom-call | tf_op jit(solution)/shard_map/slope_integral/pallas_call | solution.py:439
  185.1 1.5 multiply_add_fusion.5
  186.5 0.1 fusion.29
  186.6 1.2 fusion.1
  187.8 90.0 %slope_integral.8 = f32[4,32,16,128]{3,2,1,0:T(8,128)} custom-call(f32[2048,128]{1,0:T(8,128)} %bitcast.13, f32[8,128]{1,0:T(8,128)} %broadcast_in_dim.2.mask_ref, bf16[512,256]{1,0:T(8,128)(2,1)} %get-tuple-element.34.site_high, bf16[512,256]{1,0:T(8,128)(2,1)} %get-tuple-element.33.site_low, bf16[512,256]{1,0:T(8,128)(2,1)} %get-tuple-element.44.back_high, ...), custom_call_target="tpu_custom_call" | custom-call | tf_op jit(solution)/shard_map/slope_integral/pallas_call | solution.py:439
  277.8 1.5 multiply_add_fusion.4
  279.4 0.1 fusion.28
  279.5 1.2 fusion.3
  280.6 90.0 %slope_integral.9 = f32[4,32,16,128]{3,2,1,0:T(8,128)} custom-call(f32[2048,128]{1,0:T(8,128)} %bitcast.14, f32[8,128]{1,0:T(8,128)} %broadcast_in_dim.2.mask_ref, bf16[512,256]{1,0:T(8,128)(2,1)} %get-tuple-element.34.site_high, bf16[512,256]{1,0:T(8,128)(2,1)} %get-tuple-element.33.site_low, bf16[512,256]{1,0:T(8,128)(2,1)} %get-tuple-element.44.back_high, ...), custom_call_target="tpu_custom_call" | custom-call | tf_op jit(solution)/shard_map/slope_integral/pallas_call | solution.py:439
  370.7 1.5 multiply_add_fusion.3
  372.2 0.1 fusion.27
  372.3 0.7 copy-done.1
  373.0 1.3 multiply_add_fusion.2
  374.3 90.0 %slope_integral.10 = f32[4,32,16,128]{3,2,1,0:T(8,128)} custom-call(f32[2048,128]{1,0:T(8,128)} %bitcast.11, f32[8,128]{1,0:T(8,128)} %broadcast_in_dim.2.mask_ref, bf16[512,256]{1,0:T(8,128)(2,1)} %get-tuple-element.34.site_high, bf16[512,256]{1,0:T(8,128)(2,1)} %get-tuple-element.33.site_low, bf16[512,256]{1,0:T(8,128)(2,1)} %get-tuple-element.44.back_high, ...), custom_call_target="tpu_custom_call" | custom-call | tf_op jit(solution)/shard_map/slope_integral/pallas_call | solution.py:439
  464.3 1.6 multiply_add_fusion.1
  465.9 0.1 fusion.26
  466.0 0.7 copy-done.2
  466.7 2.3 fusion.5
  469.0 90.1 %slope_integral.11 = f32[4,32,16,128]{3,2,1,0:T(8,128)} custom-call(f32[2048,128]{1,0:T(8,128)} %bitcast.12, f32[8,128]{1,0:T(8,128)} %broadcast_in_dim.2.mask_ref, bf16[512,256]{1,0:T(8,128)(2,1)} %get-tuple-element.34.site_high, bf16[512,256]{1,0:T(8,128)(2,1)} %get-tuple-element.33.site_low, bf16[512,256]{1,0:T(8,128)(2,1)} %get-tuple-element.44.back_high, ...), custom_call_target="tpu_custom_call" | custom-call | tf_op jit(solution)/shard_map/slope_integral/pallas_call | solution.py:439
  559.1 2.0 multiply_add_fusion
  561.1 0.1 fusion.25
  561.2 2.3 fusion.7
  (19 shorter events, 0.3 us)
Async XLA Ops:
  0.0 92.2 %copy-start = (f32[4,32,16,128]{3,2,1,0:T(8,128)S(1)}, f32[4,32,16,128]{3,2,1,0:T(8,128)}, u32[]{:S(2)}) copy-start(f32[4,32,16,128]{3,2,1,0:T(8,128)} %param.5) | copy-start | bytes 3145732
  372.3 0.7 copy-start.1
  466.0 0.7 copy-start.2
  466.0 3.0 copy-start.3
  466.0 3.0 copy-start.4
  466.0 3.0 copy-start.5
